TPU v7x, 256 devices: a whole 4x4x8 slice. The times are simulated.
256 devices in a mesh: section: 16 (over y, x), slab: 16 (over z, core).
Axes of the slice: x: 4, y: 4, z: 8, core: 2. Of those that a mesh axis runs over, the one named last changes fastest.
Arguments:
- features: bfloat16 [16, 16, 32, 2, 8, 256], P('section', None, 'slab'), may hold values from -40 to 40
- vae_weight: bfloat16 [3, 3, 3, 256, 256], replicated, may hold values from -0.078125 to 0.078125
- vae_gain: float32 [256], replicated, may hold values from 0.25 to 1.75
- vae_shift: float32 [256], replicated, may hold values from -3 to 3
- vae_bias: float32 [256], replicated, may hold values from -3 to 3
- latent_weight: bfloat16 [256, 16], replicated, may hold values from -0.375 to 0.375
- latent_bias: float32 [16], replicated, may hold values from -3 to 3
- slot_clips: int32 [16, 16], replicated, may hold values from 0 to 15, each once within a row
- row_offsets: int32 [16, 16], replicated, may hold values from 0 to 112
- in_weight: bfloat16 [3, 3, 16, 320], replicated, may hold values from -0.5 to 0.5
- in_bias: float32 [320], replicated, may hold values from -3 to 3
- pos_table: bfloat16 [128, 320], replicated, may hold values from -3 to 3
- unet_gain: float32 [16, 320], P('section'), may hold values from 0.25 to 1.75
- unet_shift: float32 [16, 320], P('section'), may hold values from -3 to 3
- unet_weight: bfloat16 [16, 3, 3, 320, 320], P('section'), may hold values from -0.109375 to 0.109375
- unet_bias: float32 [16, 320], P('section'), may hold values from -3 to 3
Outputs:
- layer_outputs: bfloat16 [16, 16, 16, 16, 2, 1280], P('section', None, 'slab')
Inputs may be any that keep to these rules, and one draw needn't show every extreme that they name: Each row of slot_clips is a permutation of 0 to 15.
All inputs are finite; a program needn't handle non-finite values.
Results may differ from a plain program's by a relative error of at most 0.025.
Values may be sent and summed in bfloat16 or wider, within the bound.
A program may use at most 64 MiB of HBM per device.

v0:
```python
import jax
import jax.numpy as jnp
from jax import lax
from jax.experimental import pallas as pl
from jax.experimental.pallas import tpu as pltpu
from jax.sharding import PartitionSpec as P

BF = jnp.bfloat16
F32 = jnp.float32
MESH = pl.DeviceIdType.MESH
EPS = 1e-6
SIDE = 4
PIECE = 240


def group_matrix(used, width, group):
    a = lax.broadcasted_iota(jnp.int32, (width, width), 0)
    b = lax.broadcasted_iota(jnp.int32, (width, width), 1)
    same = (b - b % group) == (a - a % group)
    hit = jnp.logical_and(same, jnp.logical_and(a < used, b < used))
    return jnp.where(hit, 1.0, 0.0).astype(BF)


def group_stats(values, members, count):
    first = jnp.sum(jnp.sum(values, axis=0), axis=0, keepdims=True)
    second = jnp.sum(jnp.sum(values * values, axis=0), axis=0, keepdims=True)
    parts = []
    for total in (first, second):
        high = total.astype(BF).astype(F32)
        rest = total - high
        mid = rest.astype(BF).astype(F32)
        parts += [high, mid, rest - mid]
    width = values.shape[-1]
    row = lax.broadcasted_iota(jnp.int32, (8, width), 0)
    left = jnp.zeros((8, width), F32)
    for index, part in enumerate(parts):
        left = jnp.where(row == index, part, left)
    sums = jnp.dot(left.astype(BF), members, preferred_element_type=F32)
    mean = (sums[0:1] + sums[1:2] + sums[2:3]) * (1.0 / count)
    meansq = (sums[3:4] + sums[4:5] + sums[5:6]) * (1.0 / count)
    return mean, lax.rsqrt(meansq - mean * mean + EPS)


def silu(v):
    half = 0.5 * v
    return half + half * jnp.tanh(half)


def up_down(values):
    zero = jnp.zeros_like(values[:1])
    return (
        jnp.concatenate([zero, values[:-1]], axis=0),
        jnp.concatenate([values[1:], zero], axis=0),
    )


def beside(values, step, cols):
    col = lax.broadcasted_iota(jnp.int32, values.shape, 1) % cols
    edge = 0 if step == 1 else cols - 1
    return jnp.where(col == edge, 0.0, pltpu.roll(values, step % 8, 1))


def block(y, gain, shift, bias, weight, members):
    mean, inverse = group_stats(y, members, 1280)
    act = silu((y - mean) * (inverse * gain) + shift)
    above, below = (a.reshape(128, 384) for a in up_down(act))
    here = act.reshape(128, 384)
    low = lax.broadcasted_iota(jnp.int32, (128, 128), 1) < 64
    tail = jnp.where(low, above[:, 256:], pltpu.roll(here[:, 256:], 64, 1))
    pieces = (above[:, :256], here[:, :256], below[:, :256], tail, below[:, 256:])
    left = jnp.concatenate([a.astype(BF) for a in pieces], axis=1)

    def product(n):
        return jnp.dot(left, weight[:, n * 256 : (n + 1) * 256], preferred_element_type=F32)

    def joined(main, end):
        return jnp.concatenate([main, end], axis=1).reshape(16, 8, 384)

    tails = product(3)
    ends = tails[:, :128]
    before = joined(product(0), jnp.where(low, pltpu.roll(ends, 64, 1), 0.0))
    middle = joined(product(1), jnp.where(low, ends, 0.0))
    after = joined(product(2), tails[:, 128:])
    out = y + middle + beside(before, 1, 4) + beside(after, -1, 4) + bias
    return out.astype(BF)


def pack_weight(raw, packed):
    packed[960:1024, :] = jnp.zeros((64, 1024), BF)
    for tap in range(3):
        for first, count, start in ((0, 256, tap * 256), (256, 64, 768 + 64 * tap)):
            rows = slice(start, start + count)
            ends = []
            for e in range(3):
                source = raw.at[tap * 3 + e]
                packed[rows, e * 256 : (e + 1) * 256] = source[first : first + count, :256]
                ends.append(source[first : first + count, 256:])
            packed[rows, 768:896] = jnp.concatenate([ends[1], ends[0]], axis=1)
            packed[rows, 896:1024] = jnp.concatenate([ends[2], jnp.zeros_like(ends[2])], axis=1)


def encode(clip, gain, shift, bias, weight, latent_weight, latent_bias):
    members = group_matrix(256, 256, 8)
    values = clip.astype(F32).reshape(64, 8, 256)
    mean, inverse = group_stats(values, members, 4096)
    act = silu((values - mean) * (inverse * gain) + shift).reshape(32, 2, 8, 256)
    lefts = []
    for frame in range(2):
        here = act[:, frame]
        above, below = up_down(here)
        lefts.append(
            jnp.concatenate([a.reshape(256, 256).astype(BF) for a in (above, here, below)], axis=1)
        )
    both = jnp.concatenate(lefts, axis=0)
    sums = [jnp.zeros((32, 8, 256), F32)] * 2
    for e in range(3):
        shared = jnp.dot(
            lefts[0], weight[e, 0:768, :], preferred_element_type=F32
        ) + jnp.dot(lefts[0], weight[e, 768:1536, :], preferred_element_type=F32)
        own = jnp.dot(both, weight[e, 1536:2304, :], preferred_element_type=F32)
        for frame in range(2):
            part = (shared + own[frame * 256 : (frame + 1) * 256]).reshape(32, 8, 256)
            sums[frame] = sums[frame] + (part if e == 1 else beside(part, 1 - e, 8))
    values = values.reshape(32, 2, 8, 256)
    paired = []
    for frame in range(2):
        summed = (values[:, frame] + sums[frame] + bias).reshape(16, 2, 8, 256)
        paired.append(summed[:, 0] + summed[:, 1])
    stacked = jnp.stack(paired, axis=1).reshape(256, 256)
    terms = []
    for _ in range(3):
        high = stacked.astype(BF)
        terms.append(high)
        stacked = stacked - high.astype(F32)
    row = lax.broadcasted_iota(jnp.int32, (128, 256), 0)
    col = lax.broadcasted_iota(jnp.int32, (128, 256), 1)
    pick = jnp.where(col - col % 2 == 2 * row, 1.0, 0.0).astype(BF)
    total = jnp.zeros((128, 256), F32)
    for high in terms:
        total = total + jnp.dot(pick, high, preferred_element_type=F32)
    pooled = (0.25 * total).astype(BF)
    latent = jnp.dot(pooled, latent_weight, preferred_element_type=F32) + latent_bias
    return latent.astype(BF).astype(F32)


def embed(latent, offset, weight, bias, table):
    grid = latent.reshape(16, 8, 16)
    columns = (beside(grid, 1, 4), grid, beside(grid, -1, 4))
    total = jnp.zeros((128, 320), F32)
    for e in range(3):
        above, below = up_down(columns[e])
        for b, rows in enumerate((above, columns[e], below)):
            total = total + jnp.dot(
                rows.reshape(128, 16).astype(BF), weight[b * 3 + e], preferred_element_type=F32
            )
    row = lax.broadcasted_iota(jnp.int32, (16, 8, 128), 0)
    entry = lax.broadcasted_iota(jnp.int32, (16, 8, 128), 2)
    one_hot = jnp.where(entry == row + offset, 1.0, 0.0).reshape(128, 128).astype(BF)
    placed = jnp.dot(one_hot, table, preferred_element_type=F32)
    return (total + bias + placed).astype(BF)


def kernel(
    slots,
    offsets,
    features,
    vae_weight,
    vae_gain,
    vae_shift,
    vae_bias,
    latent_weight,
    latent_bias,
    in_weight,
    in_bias,
    table,
    gain,
    shift,
    bias,
    unet_weight,
    out,
    staged,
    clip,
    encoder,
    raw,
    packed,
    norms,
    first_state,
    arriving,
    leaving,
    results,
    state,
    spread,
    members,
    load_sem,
    clip_send,
    clip_recv,
    norm_send,
    norm_recv,
    ring_send,
    ring_recv,
    twin_send,
    twin_recv,
    first_send,
    state_send,
    state_recv,
    out_send,
    out_recv,
    keep_sem,
):
    section = lax.axis_index("section")
    slab = lax.axis_index("slab")
    x, y = section % SIDE, section // SIDE
    core = slab % 2
    twin = slab + 1 - 2 * core

    def at_x(step):
        return {"section": y * SIDE + (x + step + SIDE) % SIDE}

    weight_load = pltpu.make_async_copy(unet_weight, raw, load_sem.at[27])
    weight_load.start()

    def encoder_load(tap):
        a, b, e = tap // 9, (tap // 3) % 3, tap % 3
        return pltpu.make_async_copy(
            vae_weight.at[tap],
            encoder.at[e, pl.ds(a * 768 + b * 256, 256), :],
            load_sem.at[tap],
        )

    @pl.loop(0, 27)
    def _(tap):
        encoder_load(tap).start()

    barrier = pltpu.get_barrier_semaphore()

    @pl.loop(1, SIDE)
    def _(step):
        pl.semaphore_signal(barrier, 1, device_id=at_x(step), device_id_type=MESH)
        pl.semaphore_signal(
            barrier,
            1,
            device_id={"section": ((y + step) % SIDE) * SIDE + x},
            device_id_type=MESH,
        )

    @pl.loop(1, 16)
    def _(step):
        pl.semaphore_signal(
            barrier, 1, device_id={"slab": (slab + step) % 16}, device_id_type=MESH
        )

    @pl.loop(0, 16)
    def _(slot):
        staged[slot] = features[slots[section, slot]]

    members[...] = group_matrix(320, 384, 10)
    norms[x] = jnp.zeros((8, 384), F32)
    norms[x, 0:1, 0:320] = gain[...]
    norms[x, 1:2, 0:320] = shift[...]
    norms[x, 2:3, 0:320] = bias[...]
    first_state[...] = jnp.zeros((128, 384), BF)
    weight_load.wait()
    pack_weight(raw, packed.at[x])
    for other in range(1, SIDE):
        packed[(x + other) % SIDE, 960:1024, :] = jnp.zeros((64, 1024), BF)
    pl.semaphore_wait(barrier, 21)

    def clip_copy(step):
        return pltpu.make_async_remote_copy(
            src_ref=staged.at[(slab + step) % 16],
            dst_ref=clip.at[slab],
            send_sem=clip_send.at[step],
            recv_sem=clip_recv.at[step],
            device_id={"slab": (slab + step) % 16},
            device_id_type=MESH,
        )

    def clip_arrival(step):
        return pltpu.make_async_remote_copy(
            src_ref=staged.at[slab],
            dst_ref=clip.at[(slab + 16 - step) % 16],
            send_sem=clip_send.at[step],
            recv_sem=clip_recv.at[step],
            device_id={"slab": (slab + step) % 16},
            device_id_type=MESH,
        )

    @pl.loop(1, 16)
    def _(step):
        clip_copy(step).start()

    def piece(way, owner, which):
        rows = pl.ds(pl.multiple_of((way * 2 + which) * PIECE, 16), PIECE)
        return packed.at[owner, rows, :]

    def ring_copy(way, step):
        sign = 1 - 2 * way
        mine = piece(way, (x - sign * step + SIDE) % SIDE, core)
        return pltpu.make_async_remote_copy(
            src_ref=mine,
            dst_ref=mine,
            send_sem=ring_send.at[way, step],
            recv_sem=ring_recv.at[way, step],
            device_id=at_x(sign),
            device_id_type=MESH,
        )

    def ring_arrival(way, step):
        sign = 1 - 2 * way
        theirs = piece(way, (x - sign * (step + 1) + SIDE) % SIDE, core)
        return pltpu.make_async_remote_copy(
            src_ref=theirs,
            dst_ref=theirs,
            send_sem=ring_send.at[way, step],
            recv_sem=ring_recv.at[way, step],
            device_id=at_x(sign),
            device_id_type=MESH,
        )

    def twin_copy(way, step, which):
        sign = 1 - 2 * way
        block_at = piece(way, (x - sign * (step + 1) + SIDE) % SIDE, which)
        return pltpu.make_async_remote_copy(
            src_ref=block_at,
            dst_ref=block_at,
            send_sem=twin_send.at[way, step],
            recv_sem=twin_recv.at[way, step],
            device_id={"slab": twin},
            device_id_type=MESH,
        )

    def norm_copy(step, owner):
        return pltpu.make_async_remote_copy(
            src_ref=norms.at[owner],
            dst_ref=norms.at[owner],
            send_sem=norm_send.at[step],
            recv_sem=norm_recv.at[step],
            device_id=at_x(step),
            device_id_type=MESH,
        )

    for way in range(2):
        ring_copy(way, 0).start()

    @pl.loop(1, SIDE)
    def _(step):
        norm_copy(step, x).start()

    clip[slab] = staged[slab]

    @pl.loop(0, 27)
    def _(tap):
        encoder_load(tap).wait()

    @pl.loop(1, 16)
    def _(step):
        clip_arrival(step).wait_recv()

    latent = encode(
        clip[...].reshape(512, 256),
        vae_gain[...],
        vae_shift[...],
        vae_bias[...],
        encoder,
        latent_weight[...],
        latent_bias[...],
    )
    offset = offsets[section, slots[section, slab]]
    first_state[:, 0:320] = embed(latent, offset, in_weight, in_bias[...], table[...])

    def first_copy():
        return pltpu.make_async_remote_copy(
            src_ref=first_state,
            dst_ref=arriving.at[y],
            send_sem=first_send,
            recv_sem=state_recv.at[y],
            device_id={"section": x},
            device_id_type=MESH,
        )

    @pl.when(y == 0)
    def _():
        arriving[0] = first_state[...]

    @pl.when(y > 0)
    def _():
        first_copy().start()

    for step in range(3):
        for way in range(2):
            ring_arrival(way, step).wait_recv()
            if step < 2:
                ring_copy(way, step + 1).start()
            twin_copy(way, step, core).start()

    @pl.loop(1, SIDE)
    def _(step):
        norm_copy(step, (x + SIDE - step) % SIDE).wait_recv()

    for step in range(3):
        for way in range(2):
            twin_copy(way, step, 1 - core).wait_recv()

    def state_copy(turn):
        return pltpu.make_async_remote_copy(
            src_ref=leaving.at[turn],
            dst_ref=arriving.at[turn],
            send_sem=state_send.at[turn],
            recv_sem=state_recv.at[turn],
            device_id={"section": (section + SIDE) % 16},
            device_id_type=MESH,
        )

    def out_copy(index):
        turn, layer = index // SIDE, index % SIDE
        return pltpu.make_async_remote_copy(
            src_ref=results.at[index],
            dst_ref=out.at[turn * SIDE + x],
            send_sem=out_send.at[index],
            recv_sem=out_recv.at[turn * SIDE + x],
            device_id={"section": y * SIDE + layer},
            device_id_type=MESH,
        )

    def out_arrival(micro):
        return pltpu.make_async_remote_copy(
            src_ref=results.at[micro],
            dst_ref=out.at[micro],
            send_sem=out_send.at[micro],
            recv_sem=out_recv.at[micro],
            device_id={"section": y * SIDE + micro % SIDE},
            device_id_type=MESH,
        )

    def keep_copy(turn):
        index = turn * SIDE + x
        return pltpu.make_async_copy(results.at[index], out.at[index], keep_sem.at[turn])

    @pl.loop(0, 16)
    def _(index):
        turn, layer = index // SIDE, index % SIDE

        @pl.when(jnp.logical_and(layer == 0, turn + y > 0))
        def _():
            state_copy(turn).wait_recv()

        @pl.when(layer == 0)
        def _():
            state[...] = arriving[turn].astype(F32).reshape(16, 8, 384)

        result = block(
            state[...],
            norms[layer, 0:1, :],
            norms[layer, 1:2, :],
            norms[layer, 2:3, :],
            packed.at[layer],
            members[...],
        )

        @pl.when(jnp.logical_and(layer == SIDE - 1, y < SIDE - 1))
        def _():
            leaving[turn] = result.reshape(128, 384)
            state_copy(turn).start()

        result = result.astype(F32)
        state[...] = result
        for n in range(3):
            spread[n] = result[:, :, n * 128 : (n + 1) * 128].reshape(128, 128)
        cells = []
        for col in range(4):
            every = pl.ds(col, 32, stride=4)
            cells += [spread[0, every, :], spread[1, every, :], spread[2, every, :][:, :64]]
        results[index] = jnp.concatenate(cells, axis=1).astype(BF)

        @pl.when(layer == x)
        def _():
            keep_copy(turn).start()

        @pl.when(layer != x)
        def _():
            out_copy(index).start()

    @pl.loop(0, 16)
    def _(index):
        @pl.when(index % SIDE != x)
        def _():
            out_copy(index).wait_send()
            out_arrival(index).wait_recv()

    @pl.loop(0, SIDE)
    def _(turn):
        keep_copy(turn).wait()

        @pl.when(y < SIDE - 1)
        def _():
            state_copy(turn).wait_send()

    @pl.when(y > 0)
    def _():
        first_copy().wait_send()

    @pl.loop(1, 16)
    def _(step):
        clip_copy(step).wait_send()

    @pl.loop(1, SIDE)
    def _(step):
        norm_copy(step, x).wait_send()

    for step in range(3):
        for way in range(2):
            ring_copy(way, step).wait_send()
            twin_copy(way, step, core).wait_send()


def per_device(
    features,
    vae_weight,
    vae_gain,
    vae_shift,
    vae_bias,
    latent_weight,
    latent_bias,
    slot_clips,
    row_offsets,
    in_weight,
    in_bias,
    pos_table,
    unet_gain,
    unet_shift,
    unet_weight,
    unet_bias,
):
    vmem = pl.BlockSpec(memory_space=pltpu.VMEM)
    smem = pl.BlockSpec(memory_space=pltpu.SMEM)
    anywhere = pl.BlockSpec(memory_space=pl.ANY)
    dma = pltpu.SemaphoreType.DMA
    result = pl.pallas_call(
        kernel,
        out_shape=jax.ShapeDtypeStruct((16, 32, 1280), BF),
        in_specs=[smem, smem, vmem, anywhere] + [vmem] * 11 + [anywhere],
        out_specs=anywhere,
        scratch_shapes=[
            pltpu.VMEM((16, 32, 256), BF),
            pltpu.VMEM((16, 32, 256), BF),
            pltpu.VMEM((3, 2304, 256), BF),
            pltpu.VMEM((9, 320, 320), BF),
            pltpu.VMEM((SIDE, 1024, 1024), BF),
            pltpu.VMEM((SIDE, 8, 384), F32),
            pltpu.VMEM((128, 384), BF),
            pltpu.VMEM((SIDE, 128, 384), BF),
            pltpu.VMEM((SIDE, 128, 384), BF),
            pltpu.VMEM((16, 32, 1280), BF),
            pltpu.VMEM((16, 8, 384), F32),
            pltpu.VMEM((3, 128, 128), F32),
            pltpu.VMEM((384, 384), BF),
            dma((28,)),
            dma((16,)),
            dma((16,)),
            dma((SIDE,)),
            dma((SIDE,)),
            dma((2, 3)),
            dma((2, 3)),
            dma((2, 3)),
            dma((2, 3)),
            dma,
            dma((SIDE,)),
            dma((SIDE,)),
            dma((16,)),
            dma((16,)),
            dma((SIDE,)),
        ],
        compiler_params=pltpu.CompilerParams(
            collective_id=0, has_side_effects=True, vmem_limit_bytes=48 * 1024 * 1024
        ),
    )(
        slot_clips,
        row_offsets,
        features.reshape(16, 32, 256),
        vae_weight.reshape(27, 256, 256),
        vae_gain.reshape(1, 256),
        vae_shift.reshape(1, 256),
        vae_bias.reshape(1, 256),
        latent_weight,
        latent_bias.reshape(1, 16),
        in_weight.reshape(9, 16, 320),
        in_bias.reshape(1, 320),
        pos_table,
        unet_gain,
        unet_shift,
        unet_bias,
        unet_weight.reshape(9, 320, 320),
    )
    return result.reshape(1, 16, 1, 16, 2, 1280)


def solution(mesh):
    return jax.shard_map(
        per_device,
        mesh=mesh,
        in_specs=(
            P("section", None, "slab", None, None, None),
            P(),
            P(),
            P(),
            P(),
            P(),
            P(),
            P(),
            P(),
            P(),
            P(),
            P(),
            P("section", None),
            P("section", None),
            P("section", None, None, None, None),
            P("section", None),
        ),
        out_specs=P("section", None, "slab", None, None, None),
        check_vma=False,
    )
```

profile of v0, /device:TPU:30, one launch (start us, length us, event | category | flops | bytes accessed | tf_op | source)
XLA Modules:
  0.0 100.4 jit_solution(5087339069182316488)
XLA Ops:
  0.0 0.7 reshape.37.in_bias
  0.7 0.8 copy.17.latent_weight
  1.5 1.0 copy.18.table
  2.5 0.0 copy-start
  2.5 1.6 %copy-done = bf16[1,3,3,320,320]{4,3,2,1,0:T(8,128)(2,1)S(1)} copy-done((bf16[1,3,3,320,320]{4,3,2,1,0:T(8,128)(2,1)S(1)}, bf16[1,3,3,320,320]{4,3,2,1,0:T(8,128)(2,1)}, u32[]{:S(2)}) %copy-start) | copy-done | bytes 1843224
  4.1 0.0 copy-start.1
  4.1 0.9 copy-done.1
  5.1 0.0 copy-start.2
  5.1 0.9 copy-done.2
  6.0 0.0 copy-start.3
  6.0 0.7 copy-done.3
  6.7 0.0 copy-start.4
  6.7 0.7 copy-done.4
  7.4 0.0 copy-start.5
  7.4 0.7 copy-done.5
  8.1 0.7 copy-done.6
  8.7 0.0 copy-start.7
  8.7 0.7 copy-done.7
  9.4 0.7 copy-done.8
  10.1 0.7 copy-done.9
  10.8 0.7 copy-done.10
  11.5 0.7 copy-done.11
  12.1 86.9 %shard_map.154 = bf16[16,32,1280]{2,1,0:T(8,128)(2,1)S(1)} custom-call(s32[16,16]{1,0:T(8,128)S(1)} %copy-done.3, s32[16,16]{1,0:T(8,128)S(1)} %copy-done.4, bf16[16,32,256]{2,1,0:T(8,128)(2,1)S(1)} %bitcast.10, bf16[27,256,256]{2,1,0:T(8,128)(2,1)} %bitcast.16, f32[1,256]{1,0:T(1,128)S(1)} %bitcast.12, f32[1,256]{1,0:T(1,128)S(1)} %bitcast.13, ...), custom_call_target="tpu_custom_call" | custom-call | tf_op jit(solution)/shard_map/pallas_call | solution.py:538
  99.1 1.4 %reshape.39 = bf16[1,16,1,16,2,1280]{5,4,3,1,2,0:T(2,128)(2,1)} reshape(bf16[16,32,1280]{2,1,0:T(8,128)(2,1)S(1)} %shard_map.154) | data formatting | bytes 2621440 | tf_op jit(solution)/shard_map/reshape | solution.py:594
  (5 shorter events, 0.0 us)
Async XLA Ops:
  2.5 1.6 %copy-start = (bf16[1,3,3,320,320]{4,3,2,1,0:T(8,128)(2,1)S(1)}, bf16[1,3,3,320,320]{4,3,2,1,0:T(8,128)(2,1)}, u32[]{:S(2)}) copy-start(bf16[1,3,3,320,320]{4,3,2,1,0:T(8,128)(2,1)} %param.30) | copy-start | bytes 5529604
  4.1 0.9 copy-start.1
  5.1 0.9 copy-start.2
  6.0 0.7 copy-start.3
  6.7 0.7 copy-start.4
  7.4 0.7 copy-start.5
  8.1 0.7 copy-start.6
  8.7 0.7 copy-start.7
  9.4 0.7 copy-start.8
  10.1 0.7 copy-start.9
  10.8 0.7 copy-start.10
  11.5 0.7 copy-start.11
where the time goes:
time: 101 us; the launch traced here: 100 us
  Pallas kernels  86.9 us (86%)
  local copies, waits for them, and re-layouts  13.5 us (13%)
    pallas_call x1, Pallas kernels, per_device(): pl.pallas_call(kernel, out_shape=jax.ShapeDtypeStruct((16, 32, 1280), BF)...  86.9 us
    unnamed x26, local copies, waits for them, and re-layouts  11.4 us

commit v1 on v0

--- a/solution.py
+++ b/solution.py
@@ -10,7 +10,8 @@
 MESH = pl.DeviceIdType.MESH
 EPS = 1e-6
 SIDE = 4
-PIECE = 240
+QUARTER = 240
+CHUNKS = ((0, 64), (64, 64), (128, 64), (192, 48))
 
 
 def group_matrix(used, width, group):
@@ -44,6 +45,10 @@
 def silu(v):
     half = 0.5 * v
     return half + half * jnp.tanh(half)
+
+
+def across(left, right):
+    return lax.dot_general(left, right, (((1,), (1,)), ((), ())), preferred_element_type=F32)
 
 
 def up_down(values):
@@ -139,7 +144,7 @@
     for high in terms:
         total = total + jnp.dot(pick, high, preferred_element_type=F32)
     pooled = (0.25 * total).astype(BF)
-    latent = jnp.dot(pooled, latent_weight, preferred_element_type=F32) + latent_bias
+    latent = across(pooled, latent_weight) + latent_bias
     return latent.astype(BF).astype(F32)
 
 
@@ -156,15 +161,31 @@
     row = lax.broadcasted_iota(jnp.int32, (16, 8, 128), 0)
     entry = lax.broadcasted_iota(jnp.int32, (16, 8, 128), 2)
     one_hot = jnp.where(entry == row + offset, 1.0, 0.0).reshape(128, 128).astype(BF)
-    placed = jnp.dot(one_hot, table, preferred_element_type=F32)
+    placed = across(one_hot, table)
     return (total + bias + placed).astype(BF)
 
 
 def kernel(
+    slots_in,
+    offsets_in,
+    features_in,
+    vae_weight,
+    vae_gain_in,
+    vae_shift_in,
+    vae_bias_in,
+    latent_weight_in,
+    latent_bias_in,
+    in_weight_in,
+    in_bias_in,
+    table_in,
+    gain_in,
+    shift_in,
+    bias_in,
+    unet_weight,
+    out,
     slots,
     offsets,
     features,
-    vae_weight,
     vae_gain,
     vae_shift,
     vae_bias,
@@ -176,8 +197,6 @@
     gain,
     shift,
     bias,
-    unet_weight,
-    out,
     staged,
     clip,
     encoder,
@@ -192,12 +211,15 @@
     spread,
     members,
     load_sem,
+    small_sem,
     clip_send,
     clip_recv,
     norm_send,
     norm_recv,
     ring_send,
     ring_recv,
+    pair_send,
+    pair_recv,
     twin_send,
     twin_recv,
     first_send,
@@ -211,13 +233,44 @@
     slab = lax.axis_index("slab")
     x, y = section % SIDE, section // SIDE
     core = slab % 2
+    parity = (slab // 2) % 2
     twin = slab + 1 - 2 * core
 
     def at_x(step):
         return {"section": y * SIDE + (x + step + SIDE) % SIDE}
 
+    def remote(source, target, send, recv, device):
+        return pltpu.make_async_remote_copy(
+            src_ref=source,
+            dst_ref=target,
+            send_sem=send,
+            recv_sem=recv,
+            device_id=device,
+            device_id_type=MESH,
+        )
+
     weight_load = pltpu.make_async_copy(unet_weight, raw, load_sem.at[27])
-    weight_load.start()
+    small = [
+        pltpu.make_async_copy(source, target, small_sem.at[index])
+        for index, (source, target) in enumerate(
+            (
+                (slots_in, slots),
+                (offsets_in, offsets),
+                (features_in, features),
+                (gain_in, gain),
+                (shift_in, shift),
+                (bias_in, bias),
+                (vae_gain_in, vae_gain),
+                (vae_shift_in, vae_shift),
+                (vae_bias_in, vae_bias),
+                (latent_weight_in, latent_weight),
+                (latent_bias_in, latent_bias),
+                (in_weight_in, in_weight),
+                (in_bias_in, in_bias),
+                (table_in, table),
+            )
+        )
+    ]
 
     def encoder_load(tap):
         a, b, e = tap // 9, (tap // 3) % 3, tap % 3
@@ -227,120 +280,117 @@
             load_sem.at[tap],
         )
 
+    barrier = pltpu.get_barrier_semaphore()
+
+    def greet(device):
+        pl.semaphore_signal(barrier, 1, device_id=device, device_id_type=MESH)
+
+    @pl.loop(1, 16)
+    def _(step):
+        greet({"slab": (slab + step) % 16})
+
+    @pl.loop(1, SIDE)
+    def _(step):
+        greet(at_x(step))
+        greet({"section": ((y + step) % SIDE) * SIDE + x})
+
+    weight_load.start()
+    for copy in small:
+        copy.start()
+
     @pl.loop(0, 27)
     def _(tap):
         encoder_load(tap).start()
 
-    barrier = pltpu.get_barrier_semaphore()
-
-    @pl.loop(1, SIDE)
-    def _(step):
-        pl.semaphore_signal(barrier, 1, device_id=at_x(step), device_id_type=MESH)
-        pl.semaphore_signal(
-            barrier,
-            1,
-            device_id={"section": ((y + step) % SIDE) * SIDE + x},
-            device_id_type=MESH,
-        )
-
-    @pl.loop(1, 16)
-    def _(step):
-        pl.semaphore_signal(
-            barrier, 1, device_id={"slab": (slab + step) % 16}, device_id_type=MESH
-        )
+    members[...] = group_matrix(320, 384, 10)
+    first_state[...] = jnp.zeros((128, 384), BF)
+    for layer in range(SIDE):
+        packed[layer, 960:1024, :] = jnp.zeros((64, 1024), BF)
+    norms[x] = jnp.zeros((8, 384), F32)
+    weight_load.wait()
+    pack_weight(raw, packed.at[x])
+    for copy in small:
+        copy.wait()
+    norms[x, 0:1, 0:320] = gain[...]
+    norms[x, 1:2, 0:320] = shift[...]
+    norms[x, 2:3, 0:320] = bias[...]
 
     @pl.loop(0, 16)
     def _(slot):
         staged[slot] = features[slots[section, slot]]
 
-    members[...] = group_matrix(320, 384, 10)
-    norms[x] = jnp.zeros((8, 384), F32)
-    norms[x, 0:1, 0:320] = gain[...]
-    norms[x, 1:2, 0:320] = shift[...]
-    norms[x, 2:3, 0:320] = bias[...]
-    first_state[...] = jnp.zeros((128, 384), BF)
-    weight_load.wait()
-    pack_weight(raw, packed.at[x])
-    for other in range(1, SIDE):
-        packed[(x + other) % SIDE, 960:1024, :] = jnp.zeros((64, 1024), BF)
     pl.semaphore_wait(barrier, 21)
 
+    def chunk(owner, side, which, index):
+        first, count = CHUNKS[index]
+        start = (side * 2 + which) * QUARTER + first
+        return packed.at[owner, pl.ds(pl.multiple_of(start, 16), count), :]
+
+    def ring_copy(distance, index, from_left):
+        step = 1 if from_left else -1
+        owner = (x + step - distance + 2 * SIDE) % SIDE
+        mine = chunk(owner, parity, core, index)
+        at = (distance - 1) * 4 + index
+        return remote(mine, mine, ring_send.at[at], ring_recv.at[at], at_x(step))
+
+    def moved(distance, index, side, which, sems, device):
+        owner = (x - distance + SIDE) % SIDE
+        mine = chunk(owner, side, which, index)
+        at = (distance - 1) * 4 + index
+        return remote(mine, mine, sems[0].at[at], sems[1].at[at], device)
+
+    ring = (ring_send, ring_recv)
+    pair = (pair_send, pair_recv)
+    twins = [(twin_send.at[n], twin_recv.at[n]) for n in range(2)]
+
+    def along_z(index):
+        return {"slab": (slab + (2 if index < 2 else 14)) % 16}
+
+    events = [(1, 0), (3, 2), (1, 1), (3, 3), (1, 2), (3, 0), (1, 3), (3, 1), (2, 0), (2, 2), (2, 1), (2, 3)]
+    relays = {(1, 0): True, (1, 1): True, (3, 2): False, (3, 3): False}
+    own_sends = [(1, 0, True), (3, 2, False), (1, 1, True), (3, 3, False)]
+    own_sends += [(1, 2, True), (3, 0, False), (1, 3, True), (3, 1, False)]
+    ring_sends = own_sends + [(2, event[1], way) for event, way in relays.items()]
+
+    def on_ring(number):
+        distance, index = events[number]
+        moved(distance, index, parity, core, ring, at_x(1)).wait_recv()
+        if events[number] in relays:
+            ring_copy(2, index, relays[events[number]]).start()
+        moved(distance, index, parity, core, pair, along_z(index)).start()
+        moved(distance, index, parity, core, twins[0], {"slab": twin}).start()
+
+    def on_pair(number):
+        distance, index = events[number]
+        moved(distance, index, 1 - parity, core, pair, along_z(index)).wait_recv()
+        moved(distance, index, 1 - parity, core, twins[1], {"slab": twin}).start()
+
+    for distance, index, from_left in own_sends:
+        ring_copy(distance, index, from_left).start()
+
     def clip_copy(step):
-        return pltpu.make_async_remote_copy(
-            src_ref=staged.at[(slab + step) % 16],
-            dst_ref=clip.at[slab],
-            send_sem=clip_send.at[step],
-            recv_sem=clip_recv.at[step],
-            device_id={"slab": (slab + step) % 16},
-            device_id_type=MESH,
+        to = (slab + step) % 16
+        return remote(
+            staged.at[to], clip.at[slab], clip_send.at[step], clip_recv.at[step], {"slab": to}
         )
 
     def clip_arrival(step):
-        return pltpu.make_async_remote_copy(
-            src_ref=staged.at[slab],
-            dst_ref=clip.at[(slab + 16 - step) % 16],
-            send_sem=clip_send.at[step],
-            recv_sem=clip_recv.at[step],
-            device_id={"slab": (slab + step) % 16},
-            device_id_type=MESH,
+        return remote(
+            staged.at[slab],
+            clip.at[(slab + 16 - step) % 16],
+            clip_send.at[step],
+            clip_recv.at[step],
+            {"slab": (slab + step) % 16},
         )
 
     @pl.loop(1, 16)
     def _(step):
         clip_copy(step).start()
 
-    def piece(way, owner, which):
-        rows = pl.ds(pl.multiple_of((way * 2 + which) * PIECE, 16), PIECE)
-        return packed.at[owner, rows, :]
-
-    def ring_copy(way, step):
-        sign = 1 - 2 * way
-        mine = piece(way, (x - sign * step + SIDE) % SIDE, core)
-        return pltpu.make_async_remote_copy(
-            src_ref=mine,
-            dst_ref=mine,
-            send_sem=ring_send.at[way, step],
-            recv_sem=ring_recv.at[way, step],
-            device_id=at_x(sign),
-            device_id_type=MESH,
-        )
-
-    def ring_arrival(way, step):
-        sign = 1 - 2 * way
-        theirs = piece(way, (x - sign * (step + 1) + SIDE) % SIDE, core)
-        return pltpu.make_async_remote_copy(
-            src_ref=theirs,
-            dst_ref=theirs,
-            send_sem=ring_send.at[way, step],
-            recv_sem=ring_recv.at[way, step],
-            device_id=at_x(sign),
-            device_id_type=MESH,
-        )
-
-    def twin_copy(way, step, which):
-        sign = 1 - 2 * way
-        block_at = piece(way, (x - sign * (step + 1) + SIDE) % SIDE, which)
-        return pltpu.make_async_remote_copy(
-            src_ref=block_at,
-            dst_ref=block_at,
-            send_sem=twin_send.at[way, step],
-            recv_sem=twin_recv.at[way, step],
-            device_id={"slab": twin},
-            device_id_type=MESH,
-        )
-
     def norm_copy(step, owner):
-        return pltpu.make_async_remote_copy(
-            src_ref=norms.at[owner],
-            dst_ref=norms.at[owner],
-            send_sem=norm_send.at[step],
-            recv_sem=norm_recv.at[step],
-            device_id=at_x(step),
-            device_id_type=MESH,
-        )
-
-    for way in range(2):
-        ring_copy(way, 0).start()
+        return remote(
+            norms.at[owner], norms.at[owner], norm_send.at[step], norm_recv.at[step], at_x(step)
+        )
 
     @pl.loop(1, SIDE)
     def _(step):
@@ -351,6 +401,9 @@
     @pl.loop(0, 27)
     def _(tap):
         encoder_load(tap).wait()
+
+    for number in range(4):
+        on_ring(number)
 
     @pl.loop(1, 16)
     def _(step):
@@ -366,16 +419,13 @@
         latent_bias[...],
     )
     offset = offsets[section, slots[section, slab]]
-    first_state[:, 0:320] = embed(latent, offset, in_weight, in_bias[...], table[...])
+    first_state[:, 0:320] = embed(
+        latent, offset, in_weight, in_bias[...].reshape(1, 320), table[...]
+    )
 
     def first_copy():
-        return pltpu.make_async_remote_copy(
-            src_ref=first_state,
-            dst_ref=arriving.at[y],
-            send_sem=first_send,
-            recv_sem=state_recv.at[y],
-            device_id={"section": x},
-            device_id_type=MESH,
+        return remote(
+            first_state, arriving.at[y], first_send, state_recv.at[y], {"section": x}
         )
 
     @pl.when(y == 0)
@@ -386,50 +436,48 @@
     def _():
         first_copy().start()
 
-    for step in range(3):
-        for way in range(2):
-            ring_arrival(way, step).wait_recv()
-            if step < 2:
-                ring_copy(way, step + 1).start()
-            twin_copy(way, step, core).start()
+    for number in range(4, 12):
+        on_ring(number)
+        on_pair(number - 4)
+    for number in range(8, 12):
+        on_pair(number)
 
     @pl.loop(1, SIDE)
     def _(step):
         norm_copy(step, (x + SIDE - step) % SIDE).wait_recv()
 
-    for step in range(3):
-        for way in range(2):
-            twin_copy(way, step, 1 - core).wait_recv()
+    for distance, index in events:
+        for n in range(2):
+            side = parity if n == 0 else 1 - parity
+            moved(distance, index, side, 1 - core, twins[n], {"slab": twin}).wait_recv()
 
     def state_copy(turn):
-        return pltpu.make_async_remote_copy(
-            src_ref=leaving.at[turn],
-            dst_ref=arriving.at[turn],
-            send_sem=state_send.at[turn],
-            recv_sem=state_recv.at[turn],
-            device_id={"section": (section + SIDE) % 16},
-            device_id_type=MESH,
+        return remote(
+            leaving.at[turn],
+            arriving.at[turn],
+            state_send.at[turn],
+            state_recv.at[turn],
+            {"section": (section + SIDE) % 16},
         )
 
     def out_copy(index):
         turn, layer = index // SIDE, index % SIDE
-        return pltpu.make_async_remote_copy(
-            src_ref=results.at[index],
-            dst_ref=out.at[turn * SIDE + x],
-            send_sem=out_send.at[index],
-            recv_sem=out_recv.at[turn * SIDE + x],
-            device_id={"section": y * SIDE + layer},
-            device_id_type=MESH,
+        micro = turn * SIDE + x
+        return remote(
+            results.at[index],
+            out.at[micro],
+            out_send.at[index],
+            out_recv.at[micro],
+            {"section": y * SIDE + layer},
         )
 
     def out_arrival(micro):
-        return pltpu.make_async_remote_copy(
-            src_ref=results.at[micro],
-            dst_ref=out.at[micro],
-            send_sem=out_send.at[micro],
-            recv_sem=out_recv.at[micro],
-            device_id={"section": y * SIDE + micro % SIDE},
-            device_id_type=MESH,
+        return remote(
+            results.at[micro],
+            out.at[micro],
+            out_send.at[micro],
+            out_recv.at[micro],
+            {"section": y * SIDE + micro % SIDE},
         )
 
     def keep_copy(turn):
@@ -507,10 +555,13 @@
     def _(step):
         norm_copy(step, x).wait_send()
 
-    for step in range(3):
-        for way in range(2):
-            ring_copy(way, step).wait_send()
-            twin_copy(way, step, core).wait_send()
+    for distance, index, from_left in ring_sends:
+        ring_copy(distance, index, from_left).wait_send()
+    for distance, index in events:
+        moved(distance, index, parity, core, pair, along_z(index)).wait_send()
+        for n in range(2):
+            side = parity if n == 0 else 1 - parity
+            moved(distance, index, side, core, twins[n], {"slab": twin}).wait_send()
 
 
 def per_device(
@@ -531,16 +582,29 @@
     unet_weight,
     unet_bias,
 ):
-    vmem = pl.BlockSpec(memory_space=pltpu.VMEM)
-    smem = pl.BlockSpec(memory_space=pltpu.SMEM)
+    hbm = pl.BlockSpec(memory_space=pltpu.HBM)
     anywhere = pl.BlockSpec(memory_space=pl.ANY)
     dma = pltpu.SemaphoreType.DMA
     result = pl.pallas_call(
         kernel,
         out_shape=jax.ShapeDtypeStruct((16, 32, 1280), BF),
-        in_specs=[smem, smem, vmem, anywhere] + [vmem] * 11 + [anywhere],
+        in_specs=[hbm] * 16,
         out_specs=anywhere,
         scratch_shapes=[
+            pltpu.SMEM((16, 16), jnp.int32),
+            pltpu.SMEM((16, 16), jnp.int32),
+            pltpu.VMEM((16, 32, 256), BF),
+            pltpu.VMEM((1, 256), F32),
+            pltpu.VMEM((1, 256), F32),
+            pltpu.VMEM((1, 256), F32),
+            pltpu.VMEM((16, 256), BF),
+            pltpu.VMEM((1, 16), F32),
+            pltpu.VMEM((9, 16, 320), BF),
+            pltpu.VMEM((320,), F32),
+            pltpu.VMEM((320, 128), BF),
+            pltpu.VMEM((1, 320), F32),
+            pltpu.VMEM((1, 320), F32),
+            pltpu.VMEM((1, 320), F32),
             pltpu.VMEM((16, 32, 256), BF),
             pltpu.VMEM((16, 32, 256), BF),
             pltpu.VMEM((3, 2304, 256), BF),
@@ -555,14 +619,17 @@
             pltpu.VMEM((3, 128, 128), F32),
             pltpu.VMEM((384, 384), BF),
             dma((28,)),
+            dma((14,)),
             dma((16,)),
             dma((16,)),
             dma((SIDE,)),
             dma((SIDE,)),
-            dma((2, 3)),
-            dma((2, 3)),
-            dma((2, 3)),
-            dma((2, 3)),
+            dma((12,)),
+            dma((12,)),
+            dma((12,)),
+            dma((12,)),
+            dma((2, 12)),
+            dma((2, 12)),
             dma,
             dma((SIDE,)),
             dma((SIDE,)),
@@ -571,7 +638,7 @@
             dma((SIDE,)),
         ],
         compiler_params=pltpu.CompilerParams(
-            collective_id=0, has_side_effects=True, vmem_limit_bytes=48 * 1024 * 1024
+            collective_id=0, has_side_effects=True, vmem_limit_bytes=63 * 1024 * 1024
         ),
     )(
         slot_clips,
@@ -581,11 +648,11 @@
         vae_gain.reshape(1, 256),
         vae_shift.reshape(1, 256),
         vae_bias.reshape(1, 256),
-        latent_weight,
+        latent_weight.T,
         latent_bias.reshape(1, 16),
         in_weight.reshape(9, 16, 320),
-        in_bias.reshape(1, 320),
-        pos_table,
+        in_bias,
+        pos_table.T,
         unet_gain,
         unet_shift,
         unet_bias,

time: 101 us -> 78 us (0.77)
  Pallas kernels: 86.9 us -> 73.9 us
  local copies, waits for them, and re-layouts: 13.5 us -> 3.96 us
    pallas_call x1, Pallas kernels: 86.9 us -> 73.9 us  [per_device(): pl.pallas_call(kernel, out_shape=jax.ShapeDtypeStruct((16, 32, 1280), BF)...]
    unnamed x26 -> x0, local copies, waits for them, and re-layouts: 11.4 us -> none
    reshape x1, local copies, waits for them, and re-layouts: 1.36 us -> 3.96 us  [per_device(): return result.reshape(1, 16, 1, 16, 2, 1280)]
where the time goes in v1:
time: 78 us; the launch traced here: 77.9 us
  Pallas kernels  73.9 us (95%)
  local copies, waits for them, and re-layouts  3.96 us (5%)
    pallas_call x1, Pallas kernels, per_device(): pl.pallas_call(kernel, out_shape=jax.ShapeDtypeStruct((16, 32, 1280), BF)...  73.9 us
    reshape x1, local copies, waits for them, and re-layouts, per_device(): return result.reshape(1, 16, 1, 16, 2, 1280)  3.96 us

profile of v1, /device:TPU:30, one launch (start us, length us, event | category | flops | bytes accessed | tf_op | source)
XLA Modules:
  0.0 77.9 jit_solution(11268045677006408869)
XLA Ops:
  0.0 73.9 %shard_map.154 = bf16[16,32,1280]{2,1,0:T(8,128)(2,1)} custom-call(s32[16,16]{1,0:T(8,128)} %slots_in.1, s32[16,16]{1,0:T(8,128)} %offsets_in.1, bf16[16,32,256]{2,1,0:T(8,128)(2,1)} %bitcast.13, bf16[27,256,256]{2,1,0:T(8,128)(2,1)} %bitcast.11, f32[1,256]{1,0:T(1,128)} %bitcast.17, f32[1,256]{1,0:T(1,128)} %bitcast.18, f32[1,256]{1,0:T(1,128)} %bitcast.19, ...), custom_call_target="tpu_custom_call" | custom-call | tf_op jit(solution)/shard_map/pallas_call | solution.py:588
  73.9 4.0 %reshape.35 = bf16[1,16,1,16,2,1280]{5,4,3,1,2,0:T(2,128)(2,1)} reshape(bf16[16,32,1280]{2,1,0:T(8,128)(2,1)} %shard_map.154) | data formatting | bytes 2621440 | tf_op jit(solution)/shard_map/reshape | solution.py:661

commit v2 on v1

--- a/solution.py
+++ b/solution.py
@@ -22,18 +22,20 @@
     return jnp.where(hit, 1.0, 0.0).astype(BF)
 
 
-def group_stats(values, members, count):
-    first = jnp.sum(jnp.sum(values, axis=0), axis=0, keepdims=True)
-    second = jnp.sum(jnp.sum(values * values, axis=0), axis=0, keepdims=True)
+def partial_sums(values):
+    return jnp.sum(values, axis=0), jnp.sum(values * values, axis=0)
+
+
+def group_stats(partial, members, count):
     parts = []
-    for total in (first, second):
+    for eighths in partial:
+        total = jnp.sum(eighths, axis=0, keepdims=True)
         high = total.astype(BF).astype(F32)
         rest = total - high
         mid = rest.astype(BF).astype(F32)
         parts += [high, mid, rest - mid]
-    width = values.shape[-1]
-    row = lax.broadcasted_iota(jnp.int32, (8, width), 0)
-    left = jnp.zeros((8, width), F32)
+    left = jnp.zeros_like(partial[0])
+    row = lax.broadcasted_iota(jnp.int32, left.shape, 0)
     for index, part in enumerate(parts):
         left = jnp.where(row == index, part, left)
     sums = jnp.dot(left.astype(BF), members, preferred_element_type=F32)
@@ -65,8 +67,8 @@
     return jnp.where(col == edge, 0.0, pltpu.roll(values, step % 8, 1))
 
 
-def block(y, gain, shift, bias, weight, members):
-    mean, inverse = group_stats(y, members, 1280)
+def block(y, stats, gain, shift, bias, weight):
+    mean, inverse = stats
     act = silu((y - mean) * (inverse * gain) + shift)
     above, below = (a.reshape(128, 384) for a in up_down(act))
     here = act.reshape(128, 384)
@@ -78,16 +80,32 @@
     def product(n):
         return jnp.dot(left, weight[:, n * 256 : (n + 1) * 256], preferred_element_type=F32)
 
-    def joined(main, end):
-        return jnp.concatenate([main, end], axis=1).reshape(16, 8, 384)
+    def summed(before, middle, after, first, last):
+        before, middle, after = (a.reshape(16, 8, last - first) for a in (before, middle, after))
+        shifted = beside(before, 1, 4) + beside(after, -1, 4)
+        return (y[:, :, first:last] + middle + shifted + bias[:, first:last]).astype(BF)
 
     tails = product(3)
     ends = tails[:, :128]
-    before = joined(product(0), jnp.where(low, pltpu.roll(ends, 64, 1), 0.0))
-    middle = joined(product(1), jnp.where(low, ends, 0.0))
-    after = joined(product(2), tails[:, 128:])
-    out = y + middle + beside(before, 1, 4) + beside(after, -1, 4) + bias
-    return out.astype(BF)
+    high = summed(
+        jnp.where(low, pltpu.roll(ends, 64, 1), 0.0),
+        jnp.where(low, ends, 0.0),
+        tails[:, 128:],
+        256,
+        384,
+    )
+    main = summed(product(0), product(1), product(2), 0, 256)
+    return jnp.concatenate([main, high], axis=2)
+
+
+def lay_out(y, spread):
+    for n in range(3):
+        spread[n] = y[:, :, n * 128 : (n + 1) * 128].reshape(128, 128)
+    cells = []
+    for col in range(4):
+        every = pl.ds(col, 32, stride=4)
+        cells += [spread[0, every, :], spread[1, every, :], spread[2, every, :][:, :64]]
+    return jnp.concatenate(cells, axis=1).astype(BF).reshape(16, 2, 1280)
 
 
 def pack_weight(raw, packed):
@@ -107,7 +125,7 @@
 def encode(clip, gain, shift, bias, weight, latent_weight, latent_bias):
     members = group_matrix(256, 256, 8)
     values = clip.astype(F32).reshape(64, 8, 256)
-    mean, inverse = group_stats(values, members, 4096)
+    mean, inverse = group_stats(partial_sums(values), members, 4096)
     act = silu((values - mean) * (inverse * gain) + shift).reshape(32, 2, 8, 256)
     lefts = []
     for frame in range(2):
@@ -207,7 +225,7 @@
     arriving,
     leaving,
     results,
-    state,
+    kept,
     spread,
     members,
     load_sem,
@@ -285,16 +303,17 @@
     def greet(device):
         pl.semaphore_signal(barrier, 1, device_id=device, device_id_type=MESH)
 
-    @pl.loop(1, 16)
-    def _(step):
-        greet({"slab": (slab + step) % 16})
+    weight_load.start()
 
     @pl.loop(1, SIDE)
     def _(step):
         greet(at_x(step))
         greet({"section": ((y + step) % SIDE) * SIDE + x})
 
-    weight_load.start()
+    @pl.loop(1, 16)
+    def _(step):
+        greet({"slab": (slab + step) % 16})
+
     for copy in small:
         copy.start()
 
@@ -302,23 +321,10 @@
     def _(tap):
         encoder_load(tap).start()
 
-    members[...] = group_matrix(320, 384, 10)
-    first_state[...] = jnp.zeros((128, 384), BF)
     for layer in range(SIDE):
         packed[layer, 960:1024, :] = jnp.zeros((64, 1024), BF)
-    norms[x] = jnp.zeros((8, 384), F32)
     weight_load.wait()
     pack_weight(raw, packed.at[x])
-    for copy in small:
-        copy.wait()
-    norms[x, 0:1, 0:320] = gain[...]
-    norms[x, 1:2, 0:320] = shift[...]
-    norms[x, 2:3, 0:320] = bias[...]
-
-    @pl.loop(0, 16)
-    def _(slot):
-        staged[slot] = features[slots[section, slot]]
-
     pl.semaphore_wait(barrier, 21)
 
     def chunk(owner, side, which, index):
@@ -346,7 +352,7 @@
     def along_z(index):
         return {"slab": (slab + (2 if index < 2 else 14)) % 16}
 
-    events = [(1, 0), (3, 2), (1, 1), (3, 3), (1, 2), (3, 0), (1, 3), (3, 1), (2, 0), (2, 2), (2, 1), (2, 3)]
+    events = [(1, 0), (3, 2), (1, 1), (3, 3), (2, 0), (2, 2), (2, 1), (2, 3), (1, 2), (3, 0), (1, 3), (3, 1)]
     relays = {(1, 0): True, (1, 1): True, (3, 2): False, (3, 3): False}
     own_sends = [(1, 0, True), (3, 2, False), (1, 1, True), (3, 3, False)]
     own_sends += [(1, 2, True), (3, 0, False), (1, 3, True), (3, 1, False)]
@@ -365,8 +371,16 @@
         moved(distance, index, 1 - parity, core, pair, along_z(index)).wait_recv()
         moved(distance, index, 1 - parity, core, twins[1], {"slab": twin}).start()
 
-    for distance, index, from_left in own_sends:
+    for distance, index, from_left in own_sends[:4]:
         ring_copy(distance, index, from_left).start()
+
+    for copy in small:
+        copy.wait()
+
+    @pl.loop(0, 16)
+    def _(slot):
+        staged[slot] = features[slots[section, slot]]
+
 
     def clip_copy(step):
         to = (slab + step) % 16
@@ -387,6 +401,11 @@
     def _(step):
         clip_copy(step).start()
 
+    norms[x] = jnp.zeros((8, 384), F32)
+    norms[x, 0:1, 0:320] = gain[...]
+    norms[x, 1:2, 0:320] = shift[...]
+    norms[x, 2:3, 0:320] = bias[...]
+
     def norm_copy(step, owner):
         return remote(
             norms.at[owner], norms.at[owner], norm_send.at[step], norm_recv.at[step], at_x(step)
@@ -397,6 +416,8 @@
         norm_copy(step, x).start()
 
     clip[slab] = staged[slab]
+    members[...] = group_matrix(320, 384, 10)
+    first_state[...] = jnp.zeros((128, 384), BF)
 
     @pl.loop(0, 27)
     def _(tap):
@@ -404,6 +425,8 @@
 
     for number in range(4):
         on_ring(number)
+    for distance, index, from_left in own_sends[4:]:
+        ring_copy(distance, index, from_left).start()
 
     @pl.loop(1, 16)
     def _(step):
@@ -484,49 +507,50 @@
         index = turn * SIDE + x
         return pltpu.make_async_copy(results.at[index], out.at[index], keep_sem.at[turn])
 
-    @pl.loop(0, 16)
-    def _(index):
-        turn, layer = index // SIDE, index % SIDE
-
-        @pl.when(jnp.logical_and(layer == 0, turn + y > 0))
-        def _():
-            state_copy(turn).wait_recv()
-
-        @pl.when(layer == 0)
-        def _():
-            state[...] = arriving[turn].astype(F32).reshape(16, 8, 384)
-
-        result = block(
-            state[...],
-            norms[layer, 0:1, :],
-            norms[layer, 1:2, :],
-            norms[layer, 2:3, :],
-            packed.at[layer],
-            members[...],
-        )
-
-        @pl.when(jnp.logical_and(layer == SIDE - 1, y < SIDE - 1))
-        def _():
-            leaving[turn] = result.reshape(128, 384)
-            state_copy(turn).start()
-
-        result = result.astype(F32)
-        state[...] = result
-        for n in range(3):
-            spread[n] = result[:, :, n * 128 : (n + 1) * 128].reshape(128, 128)
-        cells = []
-        for col in range(4):
-            every = pl.ds(col, 32, stride=4)
-            cells += [spread[0, every, :], spread[1, every, :], spread[2, every, :][:, :64]]
-        results[index] = jnp.concatenate(cells, axis=1).astype(BF)
-
+    def push(turn, layer):
         @pl.when(layer == x)
         def _():
             keep_copy(turn).start()
 
         @pl.when(layer != x)
         def _():
-            out_copy(index).start()
+            out_copy(turn * SIDE + layer).start()
+
+    @pl.loop(0, SIDE)
+    def _(turn):
+        @pl.when(turn + y > 0)
+        def _():
+            state_copy(turn).wait_recv()
+
+        state = arriving[turn].astype(F32).reshape(16, 8, 384)
+        partial = partial_sums(state)
+        for layer in range(SIDE):
+            stats = group_stats(partial, members[...], 1280)
+            if layer > 0:
+                results[turn * SIDE + layer - 1] = lay_out(state, spread)
+            result = block(
+                state,
+                stats,
+                norms[layer, 0:1, :],
+                norms[layer, 1:2, :],
+                norms[layer, 2:3, :],
+                packed.at[layer],
+            )
+            if layer == SIDE - 1:
+
+                @pl.when(y < SIDE - 1)
+                def _():
+                    leaving[turn] = result.reshape(128, 384)
+                    state_copy(turn).start()
+
+            state = result.astype(F32)
+            partial = partial_sums(state)
+            kept[...] = state
+            state = kept[...]
+            if layer > 0:
+                push(turn, layer - 1)
+        results[turn * SIDE + SIDE - 1] = lay_out(state, spread)
+        push(turn, SIDE - 1)
 
     @pl.loop(0, 16)
     def _(index):
@@ -562,6 +586,18 @@
         for n in range(2):
             side = parity if n == 0 else 1 - parity
             moved(distance, index, side, core, twins[n], {"slab": twin}).wait_send()
+
+
+def hand_over(source, target, buffer, sems):
+    loads = [pltpu.make_async_copy(source.at[m], buffer.at[m], sems.at[0, m]) for m in range(16)]
+    stores = [pltpu.make_async_copy(buffer.at[m], target.at[m], sems.at[1, m]) for m in range(16)]
+    for copy in loads:
+        copy.start()
+    for load, store in zip(loads, stores):
+        load.wait()
+        store.start()
+    for copy in stores:
+        copy.wait()
 
 
 def per_device(
@@ -587,7 +623,7 @@
     dma = pltpu.SemaphoreType.DMA
     result = pl.pallas_call(
         kernel,
-        out_shape=jax.ShapeDtypeStruct((16, 32, 1280), BF),
+        out_shape=jax.ShapeDtypeStruct((16, 16, 2, 1280), BF),
         in_specs=[hbm] * 16,
         out_specs=anywhere,
         scratch_shapes=[
@@ -614,7 +650,7 @@
             pltpu.VMEM((128, 384), BF),
             pltpu.VMEM((SIDE, 128, 384), BF),
             pltpu.VMEM((SIDE, 128, 384), BF),
-            pltpu.VMEM((16, 32, 1280), BF),
+            pltpu.VMEM((16, 16, 2, 1280), BF),
             pltpu.VMEM((16, 8, 384), F32),
             pltpu.VMEM((3, 128, 128), F32),
             pltpu.VMEM((384, 384), BF),
@@ -658,6 +694,13 @@
         unet_bias,
         unet_weight.reshape(9, 320, 320),
     )
+    result = pl.pallas_call(
+        hand_over,
+        out_shape=jax.ShapeDtypeStruct((16, 16, 2, 1280), BF),
+        in_specs=[hbm],
+        out_specs=hbm,
+        scratch_shapes=[pltpu.VMEM((16, 16, 2, 1280), BF), dma((2, 16))],
+    )(result)
     return result.reshape(1, 16, 1, 16, 2, 1280)
 
 

time: 78 us -> 74.5 us (0.955)
  local copies, waits for them, and re-layouts: 3.96 us -> 0 us
    reshape x1 -> x0, local copies, waits for them, and re-layouts: 3.96 us -> none  [per_device(): return result.reshape(1, 16, 1, 16, 2, 1280)]
    pallas_call x1 -> x2, Pallas kernels: 73.9 us -> 74.3 us  [the longest x1 72 us: per_device(): pl.pallas_call(kernel, out_shape=jax.ShapeDtypeStruct((16, 16, 2, 1280),...]
where the time goes in v2:
time: 74.5 us; the launch traced here: 74.3 us
  Pallas kernels  74.3 us (100%)
    pallas_call x1, Pallas kernels, per_device(): pl.pallas_call(kernel, out_shape=jax.ShapeDtypeStruct((16, 16, 2, 1280),...  72 us
    pallas_call x1, Pallas kernels, per_device(): pl.pallas_call(hand_over, out_shape=jax.ShapeDtypeStruct((16, 16, 2, 1280...  2.3 us

profile of v2, /device:TPU:30, one launch (start us, length us, event | category | flops | bytes accessed | tf_op | source)
XLA Modules:
  0.0 74.3 jit_solution(2291548002730175285)
XLA Ops:
  0.0 72.0 %shard_map.154.source = bf16[16,16,2,1280]{3,2,1,0:T(2,128)(2,1)} custom-call(s32[16,16]{1,0:T(8,128)} %slots_in.1, s32[16,16]{1,0:T(8,128)} %offsets_in.1, bf16[16,32,256]{2,1,0:T(8,128)(2,1)} %bitcast.15, bf16[27,256,256]{2,1,0:T(8,128)(2,1)} %bitcast.13, f32[1,256]{1,0:T(1,128)} %bitcast.19, f32[1,256]{1,0:T(1,128)} %bitcast.20, f32[1,256]{1,0:T(1,128)} %bitcast.21, ...), custom_call_target="tpu_custom_call" | custom-call | tf_op jit(solution)/shard_map/pallas_call | solution.py:624
  72.0 2.3 %shard_map.155 = bf16[16,16,2,1280]{3,2,1,0:T(2,128)(2,1)} custom-call(bf16[16,16,2,1280]{3,2,1,0:T(2,128)(2,1)} %shard_map.154.source), custom_call_target="tpu_custom_call" | custom-call | tf_op jit(solution)/shard_map/pallas_call | solution.py:697

commit v3 on v2

--- a/solution.py
+++ b/solution.py
@@ -106,6 +106,26 @@
         every = pl.ds(col, 32, stride=4)
         cells += [spread[0, every, :], spread[1, every, :], spread[2, every, :][:, :64]]
     return jnp.concatenate(cells, axis=1).astype(BF).reshape(16, 2, 1280)
+
+
+def fold(y, target):
+    ends = y[:, 256:320]
+    target[0:128, :] = y[:, :128].astype(BF)
+    target[128:256, :] = y[:, 128:256].astype(BF)
+    target[256:320, :] = jnp.concatenate([ends[:64], ends[64:]], axis=1).astype(BF)
+
+
+def unfold(source):
+    ends = source[256:320, :].astype(F32)
+    low = lax.broadcasted_iota(jnp.int32, (64, 128), 1) < 64
+    tops = jnp.where(low, ends, 0.0)
+    bottoms = jnp.where(low, pltpu.roll(ends, 64, 1), 0.0)
+    parts = (
+        source[0:128, :].astype(F32),
+        source[128:256, :].astype(F32),
+        jnp.concatenate([tops, bottoms], axis=0),
+    )
+    return jnp.concatenate(parts, axis=1).reshape(16, 8, 384)
 
 
 def pack_weight(raw, packed):
@@ -180,7 +200,7 @@
     entry = lax.broadcasted_iota(jnp.int32, (16, 8, 128), 2)
     one_hot = jnp.where(entry == row + offset, 1.0, 0.0).reshape(128, 128).astype(BF)
     placed = across(one_hot, table)
-    return (total + bias + placed).astype(BF)
+    return total + bias + placed
 
 
 def kernel(
@@ -417,7 +437,6 @@
 
     clip[slab] = staged[slab]
     members[...] = group_matrix(320, 384, 10)
-    first_state[...] = jnp.zeros((128, 384), BF)
 
     @pl.loop(0, 27)
     def _(tap):
@@ -442,9 +461,8 @@
         latent_bias[...],
     )
     offset = offsets[section, slots[section, slab]]
-    first_state[:, 0:320] = embed(
-        latent, offset, in_weight, in_bias[...].reshape(1, 320), table[...]
-    )
+    embedded = embed(latent, offset, in_weight, in_bias[...].reshape(1, 320), table[...])
+    fold(embedded, first_state)
 
     def first_copy():
         return remote(
@@ -522,7 +540,7 @@
         def _():
             state_copy(turn).wait_recv()
 
-        state = arriving[turn].astype(F32).reshape(16, 8, 384)
+        state = unfold(arriving.at[turn])
         partial = partial_sums(state)
         for layer in range(SIDE):
             stats = group_stats(partial, members[...], 1280)
@@ -540,7 +558,7 @@
 
                 @pl.when(y < SIDE - 1)
                 def _():
-                    leaving[turn] = result.reshape(128, 384)
+                    fold(result.astype(F32).reshape(128, 384), leaving.at[turn])
                     state_copy(turn).start()
 
             state = result.astype(F32)
@@ -589,8 +607,9 @@
 
 
 def hand_over(source, target, buffer, sems):
-    loads = [pltpu.make_async_copy(source.at[m], buffer.at[m], sems.at[0, m]) for m in range(16)]
-    stores = [pltpu.make_async_copy(buffer.at[m], target.at[m], sems.at[1, m]) for m in range(16)]
+    parts = [pl.ds(n * 4, 4) for n in range(4)]
+    loads = [pltpu.make_async_copy(source.at[p], buffer.at[p], sems.at[0, n]) for n, p in enumerate(parts)]
+    stores = [pltpu.make_async_copy(buffer.at[p], target.at[p], sems.at[1, n]) for n, p in enumerate(parts)]
     for copy in loads:
         copy.start()
     for load, store in zip(loads, stores):
@@ -647,9 +666,9 @@
             pltpu.VMEM((9, 320, 320), BF),
             pltpu.VMEM((SIDE, 1024, 1024), BF),
             pltpu.VMEM((SIDE, 8, 384), F32),
-            pltpu.VMEM((128, 384), BF),
-            pltpu.VMEM((SIDE, 128, 384), BF),
-            pltpu.VMEM((SIDE, 128, 384), BF),
+            pltpu.VMEM((320, 128), BF),
+            pltpu.VMEM((SIDE, 320, 128), BF),
+            pltpu.VMEM((SIDE, 320, 128), BF),
             pltpu.VMEM((16, 16, 2, 1280), BF),
             pltpu.VMEM((16, 8, 384), F32),
             pltpu.VMEM((3, 128, 128), F32),
@@ -699,7 +718,7 @@
         out_shape=jax.ShapeDtypeStruct((16, 16, 2, 1280), BF),
         in_specs=[hbm],
         out_specs=hbm,
-        scratch_shapes=[pltpu.VMEM((16, 16, 2, 1280), BF), dma((2, 16))],
+        scratch_shapes=[pltpu.VMEM((16, 16, 2, 1280), BF), dma((2, 4))],
     )(result)
     return result.reshape(1, 16, 1, 16, 2, 1280)
 

time: 74.5 us -> 73.7 us (0.989)
  Pallas kernels: 74.3 us -> 73.5 us
where the time goes in v3:
time: 73.7 us; the launch traced here: 73.5 us
  Pallas kernels  73.5 us (100%)
    pallas_call x1, Pallas kernels, per_device(): pl.pallas_call(kernel, out_shape=jax.ShapeDtypeStruct((16, 16, 2, 1280),...  71.4 us
    pallas_call x1, Pallas kernels, per_device(): pl.pallas_call(hand_over, out_shape=jax.ShapeDtypeStruct((16, 16, 2, 1280...  2.09 us

profile of v3, /device:TPU:30, one launch (start us, length us, event | category | flops | bytes accessed | tf_op | source)
XLA Modules:
  0.0 73.5 jit_solution(6795464603998513709)
XLA Ops:
  0.0 71.4 %shard_map.154.source = bf16[16,16,2,1280]{3,2,1,0:T(2,128)(2,1)} custom-call(s32[16,16]{1,0:T(8,128)} %slots_in.1, s32[16,16]{1,0:T(8,128)} %offsets_in.1, bf16[16,32,256]{2,1,0:T(8,128)(2,1)} %bitcast.15, bf16[27,256,256]{2,1,0:T(8,128)(2,1)} %bitcast.13, f32[1,256]{1,0:T(1,128)} %bitcast.19, f32[1,256]{1,0:T(1,128)} %bitcast.20, f32[1,256]{1,0:T(1,128)} %bitcast.21, ...), custom_call_target="tpu_custom_call" | custom-call | tf_op jit(solution)/shard_map/pallas_call | solution.py:643
  71.4 2.1 %shard_map.155 = bf16[16,16,2,1280]{3,2,1,0:T(2,128)(2,1)} custom-call(bf16[16,16,2,1280]{3,2,1,0:T(2,128)(2,1)} %shard_map.154.source), custom_call_target="tpu_custom_call" | custom-call | tf_op jit(solution)/shard_map/pallas_call | solution.py:716

commit v4 on v3

--- a/solution.py
+++ b/solution.py
@@ -447,6 +447,10 @@
     for distance, index, from_left in own_sends[4:]:
         ring_copy(distance, index, from_left).start()
 
+    for number in range(4, 12):
+        on_ring(number)
+        on_pair(number - 4)
+
     @pl.loop(1, 16)
     def _(step):
         clip_arrival(step).wait_recv()
@@ -477,9 +481,6 @@
     def _():
         first_copy().start()
 
-    for number in range(4, 12):
-        on_ring(number)
-        on_pair(number - 4)
     for number in range(8, 12):
         on_pair(number)
 
@@ -570,21 +571,6 @@
         results[turn * SIDE + SIDE - 1] = lay_out(state, spread)
         push(turn, SIDE - 1)
 
-    @pl.loop(0, 16)
-    def _(index):
-        @pl.when(index % SIDE != x)
-        def _():
-            out_copy(index).wait_send()
-            out_arrival(index).wait_recv()
-
-    @pl.loop(0, SIDE)
-    def _(turn):
-        keep_copy(turn).wait()
-
-        @pl.when(y < SIDE - 1)
-        def _():
-            state_copy(turn).wait_send()
-
     @pl.when(y > 0)
     def _():
         first_copy().wait_send()
@@ -604,6 +590,21 @@
         for n in range(2):
             side = parity if n == 0 else 1 - parity
             moved(distance, index, side, core, twins[n], {"slab": twin}).wait_send()
+
+    @pl.loop(0, SIDE)
+    def _(turn):
+        keep_copy(turn).wait()
+
+        @pl.when(y < SIDE - 1)
+        def _():
+            state_copy(turn).wait_send()
+
+    @pl.loop(0, 16)
+    def _(index):
+        @pl.when(index % SIDE != x)
+        def _():
+            out_copy(index).wait_send()
+            out_arrival(index).wait_recv()
 
 
 def hand_over(source, target, buffer, sems):

time: 73.7 us -> 73.3 us (level)
  no operation moved by 1% of the time
where the time goes in v4:
time: 73.3 us; the launch traced here: 73.2 us
  Pallas kernels  73.2 us (100%)
    pallas_call x1, Pallas kernels, per_device(): pl.pallas_call(kernel, out_shape=jax.ShapeDtypeStruct((16, 16, 2, 1280),...  71.1 us
    pallas_call x1, Pallas kernels, per_device(): pl.pallas_call(hand_over, out_shape=jax.ShapeDtypeStruct((16, 16, 2, 1280...  2.09 us

profile of v4, /device:TPU:30, one launch (start us, length us, event | category | flops | bytes accessed | tf_op | source)
XLA Modules:
  0.0 73.2 jit_solution(2860210229239809440)
XLA Ops:
  0.0 71.1 %shard_map.154.source = bf16[16,16,2,1280]{3,2,1,0:T(2,128)(2,1)} custom-call(s32[16,16]{1,0:T(8,128)} %slots_in.1, s32[16,16]{1,0:T(8,128)} %offsets_in.1, bf16[16,32,256]{2,1,0:T(8,128)(2,1)} %bitcast.15, bf16[27,256,256]{2,1,0:T(8,128)(2,1)} %bitcast.13, f32[1,256]{1,0:T(1,128)} %bitcast.19, f32[1,256]{1,0:T(1,128)} %bitcast.20, f32[1,256]{1,0:T(1,128)} %bitcast.21, ...), custom_call_target="tpu_custom_call" | custom-call | tf_op jit(solution)/shard_map/pallas_call | solution.py:644
  71.1 2.1 %shard_map.155 = bf16[16,16,2,1280]{3,2,1,0:T(2,128)(2,1)} custom-call(bf16[16,16,2,1280]{3,2,1,0:T(2,128)(2,1)} %shard_map.154.source), custom_call_target="tpu_custom_call" | custom-call | tf_op jit(solution)/shard_map/pallas_call | solution.py:717

commit v5 on v4

--- a/solution.py
+++ b/solution.py
@@ -11,7 +11,8 @@
 EPS = 1e-6
 SIDE = 4
 QUARTER = 240
-CHUNKS = ((0, 64), (64, 64), (128, 64), (192, 48))
+CHUNKS = ((0, 64), (64, 48), (112, 16), (128, 64), (192, 32), (224, 16))
+FIRST = 3
 
 
 def group_matrix(used, width, group):
@@ -356,13 +357,13 @@
         step = 1 if from_left else -1
         owner = (x + step - distance + 2 * SIDE) % SIDE
         mine = chunk(owner, parity, core, index)
-        at = (distance - 1) * 4 + index
+        at = (distance - 1) * len(CHUNKS) + index
         return remote(mine, mine, ring_send.at[at], ring_recv.at[at], at_x(step))
 
     def moved(distance, index, side, which, sems, device):
         owner = (x - distance + SIDE) % SIDE
         mine = chunk(owner, side, which, index)
-        at = (distance - 1) * 4 + index
+        at = (distance - 1) * len(CHUNKS) + index
         return remote(mine, mine, sems[0].at[at], sems[1].at[at], device)
 
     ring = (ring_send, ring_recv)
@@ -370,12 +371,19 @@
     twins = [(twin_send.at[n], twin_recv.at[n]) for n in range(2)]
 
     def along_z(index):
-        return {"slab": (slab + (2 if index < 2 else 14)) % 16}
-
-    events = [(1, 0), (3, 2), (1, 1), (3, 3), (2, 0), (2, 2), (2, 1), (2, 3), (1, 2), (3, 0), (1, 3), (3, 1)]
-    relays = {(1, 0): True, (1, 1): True, (3, 2): False, (3, 3): False}
-    own_sends = [(1, 0, True), (3, 2, False), (1, 1, True), (3, 3, False)]
-    own_sends += [(1, 2, True), (3, 0, False), (1, 3, True), (3, 1, False)]
+        return {"slab": (slab + (2 if index < FIRST else 14)) % 16}
+
+    def in_turn(first, second):
+        return [event for both in zip(first, second) for event in both]
+
+    rightmost, leftmost = range(FIRST), range(FIRST, len(CHUNKS))
+    relayed = in_turn([(1, n) for n in rightmost], [(3, n) for n in leftmost])
+    opposite = in_turn([(2, n) for n in rightmost], [(2, n) for n in leftmost])
+    others = in_turn([(1, n) for n in leftmost], [(3, n) for n in rightmost])
+    events = relayed + opposite + others
+    early = len(relayed)
+    relays = {event: event[0] == 1 for event in relayed}
+    own_sends = [(distance, index, distance == 1) for distance, index in relayed + others]
     ring_sends = own_sends + [(2, event[1], way) for event, way in relays.items()]
 
     def on_ring(number):
@@ -391,7 +399,7 @@
         moved(distance, index, 1 - parity, core, pair, along_z(index)).wait_recv()
         moved(distance, index, 1 - parity, core, twins[1], {"slab": twin}).start()
 
-    for distance, index, from_left in own_sends[:4]:
+    for distance, index, from_left in own_sends[:early]:
         ring_copy(distance, index, from_left).start()
 
     for copy in small:
@@ -442,14 +450,14 @@
     def _(tap):
         encoder_load(tap).wait()
 
-    for number in range(4):
+    for number in range(early):
         on_ring(number)
-    for distance, index, from_left in own_sends[4:]:
+    for distance, index, from_left in own_sends[early:]:
         ring_copy(distance, index, from_left).start()
 
-    for number in range(4, 12):
+    for number in range(early, len(events)):
         on_ring(number)
-        on_pair(number - 4)
+        on_pair(number - early)
 
     @pl.loop(1, 16)
     def _(step):
@@ -481,7 +489,7 @@
     def _():
         first_copy().start()
 
-    for number in range(8, 12):
+    for number in range(len(events) - early, len(events)):
         on_pair(number)
 
     @pl.loop(1, SIDE)
@@ -680,12 +688,12 @@
             dma((16,)),
             dma((SIDE,)),
             dma((SIDE,)),
-            dma((12,)),
-            dma((12,)),
-            dma((12,)),
-            dma((12,)),
-            dma((2, 12)),
-            dma((2, 12)),
+            dma((18,)),
+            dma((18,)),
+            dma((18,)),
+            dma((18,)),
+            dma((2, 18)),
+            dma((2, 18)),
             dma,
             dma((SIDE,)),
             dma((SIDE,)),

time: 73.3 us -> 73 us (level)
  no operation moved by 1% of the time
where the time goes in v5:
time: 73 us; the launch traced here: 72.9 us
  Pallas kernels  72.9 us (100%)
    pallas_call x1, Pallas kernels, per_device(): pl.pallas_call(kernel, out_shape=jax.ShapeDtypeStruct((16, 16, 2, 1280),...  70.8 us
    pallas_call x1, Pallas kernels, per_device(): pl.pallas_call(hand_over, out_shape=jax.ShapeDtypeStruct((16, 16, 2, 1280...  2.09 us

profile of v5, /device:TPU:30, one launch (start us, length us, event | category | flops | bytes accessed | tf_op | source)
XLA Modules:
  0.0 72.9 jit_solution(4150470820379449772)
XLA Ops:
  0.0 70.8 %shard_map.154.source = bf16[16,16,2,1280]{3,2,1,0:T(2,128)(2,1)} custom-call(s32[16,16]{1,0:T(8,128)} %slots_in.1, s32[16,16]{1,0:T(8,128)} %offsets_in.1, bf16[16,32,256]{2,1,0:T(8,128)(2,1)} %bitcast.15, bf16[27,256,256]{2,1,0:T(8,128)(2,1)} %bitcast.13, f32[1,256]{1,0:T(1,128)} %bitcast.19, f32[1,256]{1,0:T(1,128)} %bitcast.20, f32[1,256]{1,0:T(1,128)} %bitcast.21, ...), custom_call_target="tpu_custom_call" | custom-call | tf_op jit(solution)/shard_map/pallas_call | solution.py:652
  70.8 2.1 %shard_map.155 = bf16[16,16,2,1280]{3,2,1,0:T(2,128)(2,1)} custom-call(bf16[16,16,2,1280]{3,2,1,0:T(2,128)(2,1)} %shard_map.154.source), custom_call_target="tpu_custom_call" | custom-call | tf_op jit(solution)/shard_map/pallas_call | solution.py:725
